TPU v7x, 256 devices: a whole 4x4x8 slice. The times are simulated.
256 devices in a mesh: row: 16 (over x_lo, z), col: 16 (over x_hi, y, core).
Axes of the slice: x: 4 (x_hi: 2, x_lo: 2; x = x_hi * 2 + x_lo), y: 4, z: 8, core: 2. Of those that a mesh axis runs over, the one named last changes fastest.
Arguments:
- features: bfloat16 [32768, 1024], P(('row', 'col')), may hold values from -6 to 6
- weight: bfloat16 [1024, 1024], replicated, may hold values from -0.1875 to 0.1875
- cotangent: bfloat16 [32768, 1024], P(('col', 'row')), may hold values from -6 to 6
- tile_values: bfloat16 [16, 16, 64, 128, 128], P('row', 'col'), may hold values from -0.1875 to 0.1875
- block_row: int32 [16, 16, 64], P('row', 'col'), may hold values from 0 to 15, as said below
- block_column: int32 [16, 16, 64], P('row', 'col'), may hold values from 0 to 15, as said below
- tile_count: int32 [16, 16], P('row', 'col'), may hold values from 16 to 64, as said below
Outputs:
- activated: bfloat16 [32768, 1024], P(('col', 'row'))
- feat_grad: bfloat16 [32768, 1024], P(('row', 'col'))
- weight_grad: float32 [1024, 1024], replicated
Inputs may be any that keep to these rules, and one draw needn't show every extreme that they name: `block_row`: within one grid position the slots name distinct region cells. `block_column`: within one grid position the slots name distinct region cells. `tile_count`: some grid position has exactly 64 live slots.
All inputs are finite; a program needn't handle non-finite values.
Results may differ from a plain program's by a relative error of at most 0.02.
Values may be sent and summed in bfloat16 or wider, within the bound.
A program may use at most 128 MiB of HBM per device.

v0:
```python
import jax
import jax.numpy as jnp
from jax import lax
from jax.sharding import PartitionSpec as P


def silu_slope(hidden):
    sigmoid = jax.nn.sigmoid(hidden)
    return sigmoid * (1.0 + hidden * (1.0 - sigmoid))


def spread_tiles(source, tile_block, index_in, index_out, live_count, out_blocks, flipped):
    block_size = tile_block.shape[-1]
    width = source.shape[-1]
    blocks = source.reshape(-1, block_size, width)
    per_turn = 16
    form = "tba,tbf->taf" if flipped else "tab,tbf->taf"

    def add_turn(turn, summed):
        first = turn * per_turn
        matrix = lax.dynamic_slice_in_dim(tile_block, first, per_turn, 0)
        wanted = lax.dynamic_slice_in_dim(index_in, first, per_turn, 0)
        placed = lax.dynamic_slice_in_dim(index_out, first, per_turn, 0)
        is_live = first + jnp.arange(per_turn, dtype=jnp.int32) < live_count
        picked = blocks[wanted]
        products = jnp.einsum(form, matrix, picked, preferred_element_type=jnp.float32)
        products = products * is_live.astype(jnp.float32)[:, None, None]
        return summed.at[placed].add(products)

    turns = (live_count + per_turn - 1) // per_turn
    summed = lax.fori_loop(
        0, turns, add_turn, jnp.zeros((out_blocks, block_size, width), jnp.float32)
    )
    return summed.reshape(out_blocks * block_size, width)


def on_device(features, weight, cotangent, tile_values, block_row, block_column, tile_count):
    row_devices = lax.axis_size("row")
    col_devices = lax.axis_size("col")
    span = features.shape[0]
    block_size = tile_values.shape[-1]
    per_device = span // block_size
    tile_block = tile_values[0, 0]
    rows_index = block_row[0, 0]
    cols_index = block_column[0, 0]
    live_count = tile_count[0, 0]
    projected = jnp.dot(features, weight, preferred_element_type=jnp.float32).astype(jnp.bfloat16)
    gathered = lax.all_gather(projected, "col", axis=0, tiled=True)
    partial_value = spread_tiles(
        gathered, tile_block, cols_index, rows_index, live_count, row_devices * per_device, False
    )
    hidden = lax.psum_scatter(
        partial_value.astype(jnp.bfloat16), "row", scatter_dimension=0, tiled=True
    ).astype(jnp.float32)
    activated = jax.nn.silu(hidden).astype(jnp.bfloat16)
    hidden_grad = (cotangent.astype(jnp.float32) * silu_slope(hidden)).astype(jnp.bfloat16)
    grad_group = lax.all_gather(hidden_grad, "row", axis=0, tiled=True)
    back_partial = spread_tiles(
        grad_group, tile_block, rows_index, cols_index, live_count, col_devices * per_device, True
    )
    feat_delta = lax.psum_scatter(
        back_partial.astype(jnp.bfloat16), "col", scatter_dimension=0, tiled=True
    )
    feat_grad = jnp.dot(feat_delta, weight.T, preferred_element_type=jnp.float32).astype(
        jnp.bfloat16
    )
    weight_terms = lax.dot_general(
        features, feat_delta, (((0,), (0,)), ((), ())), preferred_element_type=jnp.float32
    )
    factor = (span * row_devices * col_devices) ** (-0.5)
    weight_grad = lax.psum(weight_terms, ("row", "col")) * factor
    return (activated, feat_grad, weight_grad)


def solution(mesh):
    return jax.shard_map(
        on_device,
        mesh=mesh,
        in_specs=(
            P(("row", "col"), None),
            P(),
            P(("col", "row"), None),
            P("row", "col", None, None, None),
            P("row", "col", None),
            P("row", "col", None),
            P("row", "col"),
        ),
        out_specs=(P(("col", "row"), None), P(("row", "col"), None), P()),
        check_vma=False,
    )
```

profile of v0, /device:TPU:2, one launch (start us, length us, event | category | flops | bytes accessed | tf_op | source)
XLA Modules:
  0.0 871.9 jit_solution(16505086763936700742)
XLA Ops:
  7.2 0.0 copy-start
  7.2 0.0 all-gather.3.cloned.1.call-start
  7.2 1.5 copy-done
  8.8 2.1 convolution_convert_fusion.1
  10.9 0.0 all-gather.3.cloned.1.call-update
  10.9 0.0 reduce-scatter.3.cloned.1.call-start
  11.6 61.6 %all-gather.3.cloned.1.call-done = bf16[2048,1024]{1,0:T(8,128)(2,1)} async-done(((bf16[128,1024]{1,0:T(8,128)(2,1)}), bf16[2048,1024]{1,0:T(8,128)(2,1)}) %all-gather.3.cloned.1.call-update) | async-done | bytes 4194320 | tf_op jit(solution)/shard_map/all_gather | solution.py:48
  73.2 0.0 copy-start.4
  73.2 0.0 copy-start.5
  73.2 4.3 broadcast.35.clone
  77.5 0.0 copy-done.4
  77.6 0.0 copy-done.5
  77.6 30.5 %while.20 = (s32[]{:T(128)}, f32[16,128,1024]{2,1,0:T(8,128)}, s32[]{:T(128)}, s32[64]{0:T(128)S(1)}, bf16[64,128,128]{2,1,0:T(8,128)(2,1)}, /*index=5*/s32[64]{...) while((s32[]{:T(128)}, f32[16,128,1024]{2,1,0:T(8,128)}, ...), condition=%wide.region_2.3_spmd, body=%wide.region_0.2_spmd.sunk | while | flops 541066368 | bytes 46666480 | solution.py:31
  77.6 0.6 compare_convert_fusion.4
  78.2 0.1 compare_select_fusion.6
  78.3 5.0 gather_fusion
  83.3 6.8 broadcast_multiply_fusion.5
  90.1 17.9 %scatter_fusion = f32[16,128,1024]{2,1,0:T(8,128)} fusion(f32[16,128,1024]{2,1,0:T(8,128)} %get-tuple-element.261, s32[16]{0:T(128)S(1)} %get-tuple-element.236, f32[16,128,1024]{2,1,0:T(8,128)} %broadcast_multiply_fusion.5), kind=kCustom, calls=%fused_computation.2.clone.1 | custom fusion | flops 2097152 | bytes 25165888 | tf_op jit(solution)/shard_map/while/body/scatter-add | solution.py:28
  108.0 6.1 convert_element_type.45
  114.1 0.0 copy-start.3
  114.1 0.0 reduce-scatter.3.cloned.1.call-update
  114.1 0.0 all-gather.5.cloned.1.call-start
  114.2 171.5 %reduce-scatter.3.cloned.1.call-done = bf16[128,1024]{1,0:T(8,128)(2,1)} async-done(((bf16[2048,1024]{1,0:T(8,128)(2,1)}), bf16[128,1024]{1,0:T(8,128)(2,1)}) %reduce-scatter.3.cloned.1.call-update) | async-done | bytes 262160 | tf_op jit(solution)/shard_map/reduce_scatter | solution.py:52
  285.6 0.0 copy-done.3
  285.6 2.0 fusion.11
  287.6 0.0 all-gather.5.cloned.1.call-update
  287.7 0.0 reduce-scatter.5.cloned.1.call-start
  287.7 4.1 copy.10
  291.8 68.7 %all-gather.5.cloned.1.call-done = bf16[2048,1024]{1,0:T(8,128)(2,1)} async-done(((bf16[128,1024]{1,0:T(8,128)(2,1)}), bf16[2048,1024]{1,0:T(8,128)(2,1)}) %all-gather.5.cloned.1.call-update) | async-done | bytes 4194320 | tf_op jit(solution)/shard_map/all_gather | solution.py:57
  360.5 4.3 broadcast.35
  364.7 30.7 %while.21 = (s32[]{:T(128)}, f32[16,128,1024]{2,1,0:T(8,128)}, s32[]{:T(128)}, s32[64]{0:T(128)S(1)}, bf16[64,128,128]{1,2,0:T(8,128)(2,1)}, /*index=5*/s32[64]{...) while((s32[]{:T(128)}, f32[16,128,1024]{2,1,0:T(8,128)}, ...), condition=%wide.region_6.7_spmd, body=%wide.region_4.6_spmd.sunk | while | flops 541066368 | bytes 46666480 | solution.py:31
  364.7 0.6 compare_convert_fusion.5
  365.4 0.1 compare_select_fusion.7
  365.5 5.0 gather_fusion.1
  370.5 6.8 broadcast_multiply_fusion.6
  377.3 18.1 %scatter_fusion.1 = f32[16,128,1024]{2,1,0:T(8,128)} fusion(f32[16,128,1024]{2,1,0:T(8,128)} %get-tuple-element.297, s32[16]{0:T(128)S(1)} %get-tuple-element.246, f32[16,128,1024]{2,1,0:T(8,128)} %broadcast_multiply_fusion.6), kind=kCustom, calls=%fused_computation.3.clone.1 | custom fusion | flops 2097152 | bytes 25165888 | tf_op jit(solution)/shard_map/while/body/scatter-add | solution.py:28
  395.4 6.1 convert_element_type.51
  401.5 0.0 reduce-scatter.5.cloned.1.call-update
  401.5 0.0 all-reduce.2.cloned.1.call-start
  401.5 177.7 %reduce-scatter.5.cloned.1.call-done = bf16[128,1024]{1,0:T(8,128)(2,1)} async-done(((bf16[2048,1024]{1,0:T(8,128)(2,1)}), bf16[128,1024]{1,0:T(8,128)(2,1)}) %reduce-scatter.5.cloned.1.call-update) | async-done | bytes 262160 | tf_op jit(solution)/shard_map/reduce_scatter | solution.py:61
  579.2 0.0 copy-done.1
  579.2 3.8 convolution_bitcast_fusion
  583.0 0.0 all-reduce.2.cloned.1.call-update
  583.0 0.0 copy-done.2
  583.0 1.5 convolution_convert_fusion
  584.6 270.4 %all-reduce.2.cloned.1.call-done = f32[1024,1024]{0,1:T(8,128)} async-done(((f32[1024,1024]{0,1:T(8,128)}), f32[1024,1024]{0,1:T(8,128)}) %all-reduce.2.cloned.1.call-update) | async-done | bytes 4194320 | tf_op jit(solution)/shard_map/psum | solution.py:71
  855.0 5.1 broadcast_multiply_fusion.2
  860.1 5.3 copy.12
  (4 shorter events, 0.0 us)
Async XLA Ops:
  7.2 1.6 copy-start
  7.2 66.1 %all-gather.3.cloned.1.call-start = ((), (), s32[]{:S(2)}) async-start(), calls=%async_computation.2 | async-start | bytes 4456448 | tf_op jit(solution)/shard_map/all_gather | solution.py:48
  10.9 274.8 %reduce-scatter.3.cloned.1.call-start = ((), (), s32[]{:S(2)}) async-start(), calls=%async_computation.3 | async-start | bytes 4456448 | tf_op jit(solution)/shard_map/reduce_scatter | solution.py:52
  73.2 4.3 copy-start.4
  73.2 4.3 copy-start.5
  114.1 171.6 %copy-start.3 = (bf16[128,1024]{1,0:T(8,128)(2,1)S(1)}, bf16[128,1024]{1,0:T(8,128)(2,1)}, u32[]{:S(2)}) copy-start(bf16[128,1024]{1,0:T(8,128)(2,1)} %param.13) | copy-start | bytes 786436
  114.1 246.4 %all-gather.5.cloned.1.call-start = ((), (), s32[]{:S(2)}) async-start(), calls=%async_computation.4 | async-start | bytes 4456448 | tf_op jit(solution)/shard_map/all_gather | solution.py:57
  287.7 291.6 %reduce-scatter.5.cloned.1.call-start = ((), (), s32[]{:S(2)}) async-start(), calls=%async_computation.5 | async-start | bytes 4456448 | tf_op jit(solution)/shard_map/reduce_scatter | solution.py:61
  401.5 177.8 %copy-start.1 = (bf16[128,1024]{1,0:T(8,128)(2,1)S(1)}, bf16[128,1024]{1,0:T(8,128)(2,1)}, u32[]{:S(2)}) copy-start(bf16[128,1024]{1,0:T(8,128)(2,1)} %param.11) | copy-start | bytes 786436
  401.5 453.5 %all-reduce.2.cloned.1.call-start = ((), (), s32[]{:S(2)}) async-start(), calls=%async_computation.6 | async-start | bytes 8388608 | tf_op jit(solution)/shard_map/psum | solution.py:71
  579.2 3.8 copy-start.2
Sparse Core Ops, SparseCore 0:
  11.3 61.8 all-gather.2
  114.2 171.3 reduce-scatter.2
  288.0 72.3 all-gather.4
  401.6 177.5 reduce-scatter.4
  585.1 269.8 all-reduce.1
where the time goes:
time: 873 us; the launch traced here: 872 us
  waiting for transfers between devices  750 us (86%)
  other arithmetic  56.6 us (6%)
  local copies, waits for them, and re-layouts  29.6 us (3%)
  matrix products  21 us (2%)
  between operations  14.5 us (2%)
    psum x1, waiting for transfers between devices, on_device(): weight_grad = lax.psum(weight_terms, ('row', 'col')) * factor  270 us
    reduce_scatter x1, waiting for transfers between devices, on_device(): lax.psum_scatter(back_partial.astype(jnp.bfloat16), 'col', scatter_dimens...  178 us
    reduce_scatter x1, waiting for transfers between devices, on_device(): lax.psum_scatter(partial_value.astype(jnp.bfloat16), 'row', scatter_dimen...  171 us
    all_gather x1, waiting for transfers between devices, on_device(): grad_group = lax.all_gather(hidden_grad, 'row', axis=0, tiled=True)  68.7 us
    all_gather x1, waiting for transfers between devices, on_device(): gathered = lax.all_gather(projected, 'col', axis=0, tiled=True)  61.6 us
    scatter-add x2, other arithmetic, add_turn(): return summed.at[placed].add(products)  35.9 us
  transfers between devices with their start and end apart: 5, of which 5 were waited for; matrix products, arithmetic and copies ran while one was open for 1% of the time, Pallas kernels for 0%

commit v1 on v0

--- a/solution.py
+++ b/solution.py
@@ -68,7 +68,7 @@
         features, feat_delta, (((0,), (0,)), ((), ())), preferred_element_type=jnp.float32
     )
     factor = (span * row_devices * col_devices) ** (-0.5)
-    weight_grad = lax.psum(weight_terms, ("row", "col")) * factor
+    weight_grad = lax.psum(lax.psum(weight_terms, "row"), "col") * factor
     return (activated, feat_grad, weight_grad)
 
 

time: 873 us -> 911 us (1.044)
  waiting for transfers between devices: 750 us -> 786 us
    psum x1 -> x2, waiting for transfers between devices: 270 us -> 307 us  [on_device(): weight_grad = lax.psum(lax.psum(weight_terms, 'row'), 'col') * factor]
  transfers between devices with their start and end apart: 5 -> 6, of which waited for: 5 -> 6; matrix products, arithmetic and copies ran while one was open for 1% -> 1% of each run, Pallas kernels for 0% -> 0%
where the time goes in v1:
time: 911 us; the launch traced here: 909 us
  waiting for transfers between devices  786 us (86%)
  other arithmetic  56.6 us (6%)
  local copies, waits for them, and re-layouts  29.6 us (3%)
  matrix products  21 us (2%)
  between operations  14.8 us (2%)
    psum x2, waiting for transfers between devices, on_device(): weight_grad = lax.psum(lax.psum(weight_terms, 'row'), 'col') * factor  307 us
    reduce_scatter x1, waiting for transfers between devices, on_device(): lax.psum_scatter(back_partial.astype(jnp.bfloat16), 'col', scatter_dimens...  178 us
    reduce_scatter x1, waiting for transfers between devices, on_device(): lax.psum_scatter(partial_value.astype(jnp.bfloat16), 'row', scatter_dimen...  171 us
    all_gather x1, waiting for transfers between devices, on_device(): grad_group = lax.all_gather(hidden_grad, 'row', axis=0, tiled=True)  68.7 us
    all_gather x1, waiting for transfers between devices, on_device(): gathered = lax.all_gather(projected, 'col', axis=0, tiled=True)  61.6 us
    scatter-add x2, other arithmetic, add_turn(): return summed.at[placed].add(products)  35.9 us
  transfers between devices with their start and end apart: 6, of which 6 were waited for; matrix products, arithmetic and copies ran while one was open for 1% of the time, Pallas kernels for 0%

profile of v1, /device:TPU:2, one launch (start us, length us, event | category | flops | bytes accessed | tf_op | source)
XLA Modules:
  0.0 908.7 jit_solution(16452895451050484518)
XLA Ops:
  7.2 0.0 copy-start
  7.2 0.0 all-gather.3.cloned.1.call-start
  7.2 1.5 copy-done
  8.8 2.1 convolution_convert_fusion.1
  10.9 0.0 all-gather.3.cloned.1.call-update
  10.9 0.0 reduce-scatter.3.cloned.1.call-start
  11.6 61.6 %all-gather.3.cloned.1.call-done = bf16[2048,1024]{1,0:T(8,128)(2,1)} async-done(((bf16[128,1024]{1,0:T(8,128)(2,1)}), bf16[2048,1024]{1,0:T(8,128)(2,1)}) %all-gather.3.cloned.1.call-update) | async-done | bytes 4194320 | tf_op jit(solution)/shard_map/all_gather | solution.py:48
  73.2 4.3 broadcast.35.clone
  77.5 0.0 copy-done.4
  77.6 0.0 copy-done.5
  77.6 30.5 %while.20 = (s32[]{:T(128)}, f32[16,128,1024]{2,1,0:T(8,128)}, s32[]{:T(128)}, s32[64]{0:T(128)S(1)}, bf16[64,128,128]{2,1,0:T(8,128)(2,1)}, /*index=5*/s32[64]{...) while((s32[]{:T(128)}, f32[16,128,1024]{2,1,0:T(8,128)}, ...), condition=%wide.region_2.3_spmd, body=%wide.region_0.2_spmd.sunk | while | flops 541066368 | bytes 46666480 | solution.py:31
  77.6 0.6 compare_convert_fusion.4
  78.2 0.1 compare_select_fusion.6
  78.3 5.0 gather_fusion
  83.3 6.8 broadcast_multiply_fusion.5
  90.1 17.9 %scatter_fusion = f32[16,128,1024]{2,1,0:T(8,128)} fusion(f32[16,128,1024]{2,1,0:T(8,128)} %get-tuple-element.261, s32[16]{0:T(128)S(1)} %get-tuple-element.236, f32[16,128,1024]{2,1,0:T(8,128)} %broadcast_multiply_fusion.5), kind=kCustom, calls=%fused_computation.2.clone.1 | custom fusion | flops 2097152 | bytes 25165888 | tf_op jit(solution)/shard_map/while/body/scatter-add | solution.py:28
  108.0 6.1 convert_element_type.45
  114.1 0.0 reduce-scatter.3.cloned.1.call-update
  114.1 0.0 all-gather.5.cloned.1.call-start
  114.2 171.5 %reduce-scatter.3.cloned.1.call-done = bf16[128,1024]{1,0:T(8,128)(2,1)} async-done(((bf16[2048,1024]{1,0:T(8,128)(2,1)}), bf16[128,1024]{1,0:T(8,128)(2,1)}) %reduce-scatter.3.cloned.1.call-update) | async-done | bytes 262160 | tf_op jit(solution)/shard_map/reduce_scatter | solution.py:52
  285.6 0.0 copy-done.3
  285.6 2.0 fusion.11
  287.6 0.0 all-gather.5.cloned.1.call-update
  287.7 0.0 reduce-scatter.5.cloned.1.call-start
  287.7 4.1 copy.10
  291.8 68.7 %all-gather.5.cloned.1.call-done = bf16[2048,1024]{1,0:T(8,128)(2,1)} async-done(((bf16[128,1024]{1,0:T(8,128)(2,1)}), bf16[2048,1024]{1,0:T(8,128)(2,1)}) %all-gather.5.cloned.1.call-update) | async-done | bytes 4194320 | tf_op jit(solution)/shard_map/all_gather | solution.py:57
  360.5 4.3 broadcast.35
  364.7 30.7 %while.21 = (s32[]{:T(128)}, f32[16,128,1024]{2,1,0:T(8,128)}, s32[]{:T(128)}, s32[64]{0:T(128)S(1)}, bf16[64,128,128]{1,2,0:T(8,128)(2,1)}, /*index=5*/s32[64]{...) while((s32[]{:T(128)}, f32[16,128,1024]{2,1,0:T(8,128)}, ...), condition=%wide.region_6.7_spmd, body=%wide.region_4.6_spmd.sunk | while | flops 541066368 | bytes 46666480 | solution.py:31
  364.7 0.6 compare_convert_fusion.5
  365.4 0.1 compare_select_fusion.7
  365.5 5.0 gather_fusion.1
  370.5 6.8 broadcast_multiply_fusion.6
  377.3 18.1 %scatter_fusion.1 = f32[16,128,1024]{2,1,0:T(8,128)} fusion(f32[16,128,1024]{2,1,0:T(8,128)} %get-tuple-element.297, s32[16]{0:T(128)S(1)} %get-tuple-element.246, f32[16,128,1024]{2,1,0:T(8,128)} %broadcast_multiply_fusion.6), kind=kCustom, calls=%fused_computation.3.clone.1 | custom fusion | flops 2097152 | bytes 25165888 | tf_op jit(solution)/shard_map/while/body/scatter-add | solution.py:28
  395.4 6.1 convert_element_type.51
  401.5 0.0 reduce-scatter.5.cloned.1.call-update
  401.5 0.0 all-reduce.3.cloned.1.call-start
  401.5 177.7 %reduce-scatter.5.cloned.1.call-done = bf16[128,1024]{1,0:T(8,128)(2,1)} async-done(((bf16[2048,1024]{1,0:T(8,128)(2,1)}), bf16[128,1024]{1,0:T(8,128)(2,1)}) %reduce-scatter.5.cloned.1.call-update) | async-done | bytes 262160 | tf_op jit(solution)/shard_map/reduce_scatter | solution.py:61
  579.2 0.0 copy-done.1
  579.2 3.7 convolution_bitcast_fusion
  582.9 0.0 all-reduce.3.cloned.1.call-update
  582.9 0.0 all-reduce.5.cloned.1.call-start
  583.0 153.5 %all-reduce.3.cloned.1.call-done = f32[1024,1024]{0,1:T(8,128)} async-done(((f32[1024,1024]{0,1:T(8,128)}), f32[1024,1024]{0,1:T(8,128)}) %all-reduce.3.cloned.1.call-update) | async-done | bytes 4194320 | tf_op jit(solution)/shard_map/psum | solution.py:71
  736.5 0.0 all-reduce.5.cloned.1.call-update
  736.5 0.0 copy-done.2
  736.5 1.5 convolution_convert_fusion
  738.1 153.4 %all-reduce.5.cloned.1.call-done = f32[1024,1024]{0,1:T(8,128)} async-done(((f32[1024,1024]{0,1:T(8,128)}), f32[1024,1024]{0,1:T(8,128)}) %all-reduce.5.cloned.1.call-update) | async-done | bytes 4194320 | tf_op jit(solution)/shard_map/psum | solution.py:71
  891.4 5.1 broadcast_multiply_fusion.2
  896.5 5.3 copy.12
  (7 shorter events, 0.0 us)
Async XLA Ops:
  7.2 1.6 copy-start
  7.2 66.1 %all-gather.3.cloned.1.call-start = ((), (), s32[]{:S(2)}) async-start(), calls=%async_computation.2 | async-start | bytes 4456448 | tf_op jit(solution)/shard_map/all_gather | solution.py:48
  10.9 274.8 %reduce-scatter.3.cloned.1.call-start = ((), (), s32[]{:S(2)}) async-start(), calls=%async_computation.3 | async-start | bytes 4456448 | tf_op jit(solution)/shard_map/reduce_scatter | solution.py:52
  73.2 4.3 copy-start.4
  73.2 4.3 copy-start.5
  114.1 171.6 %copy-start.3 = (bf16[128,1024]{1,0:T(8,128)(2,1)S(1)}, bf16[128,1024]{1,0:T(8,128)(2,1)}, u32[]{:S(2)}) copy-start(bf16[128,1024]{1,0:T(8,128)(2,1)} %param.13) | copy-start | bytes 786436
  114.1 246.4 %all-gather.5.cloned.1.call-start = ((), (), s32[]{:S(2)}) async-start(), calls=%async_computation.4 | async-start | bytes 4456448 | tf_op jit(solution)/shard_map/all_gather | solution.py:57
  287.7 291.6 %reduce-scatter.5.cloned.1.call-start = ((), (), s32[]{:S(2)}) async-start(), calls=%async_computation.5 | async-start | bytes 4456448 | tf_op jit(solution)/shard_map/reduce_scatter | solution.py:61
  401.5 177.8 %copy-start.1 = (bf16[128,1024]{1,0:T(8,128)(2,1)S(1)}, bf16[128,1024]{1,0:T(8,128)(2,1)}, u32[]{:S(2)}) copy-start(bf16[128,1024]{1,0:T(8,128)(2,1)} %param.11) | copy-start | bytes 786436
  401.5 335.0 %all-reduce.3.cloned.1.call-start = ((), (), s32[]{:S(2)}) async-start(), calls=%async_computation.6 | async-start | bytes 8388608 | tf_op jit(solution)/shard_map/psum | solution.py:71
  582.9 153.6 %copy-start.2 = (bf16[128,1024]{1,0:T(8,128)(2,1)S(1)}, bf16[128,1024]{1,0:T(8,128)(2,1)}, u32[]{:S(2)}) copy-start(bf16[128,1024]{1,0:T(8,128)(2,1)} %reduce-scatter.5.cloned.1.call-done) | copy-start | bytes 786436
  582.9 308.5 %all-reduce.5.cloned.1.call-start = ((), (), s32[]{:S(2)}) async-start(), calls=%async_computation.7 | async-start | bytes 8388608 | tf_op jit(solution)/shard_map/psum | solution.py:71
Sparse Core Ops, SparseCore 0:
  11.3 61.8 all-gather.2
  114.2 171.3 reduce-scatter.2
  288.0 72.3 all-gather.4
  401.6 177.5 reduce-scatter.4
  583.1 153.3 all-reduce.2
  739.0 152.3 all-reduce.4
